TPU v7x, 128 devices: a whole 4x4x4 slice. The times are simulated.
128 devices in a mesh: side: 2 (over core), grp: 8 (over x_hi, y), tp: 8 (over x_lo, z).
Axes of the slice: x: 4 (x_hi: 2, x_lo: 2; x = x_hi * 2 + x_lo), y: 4, z: 4, core: 2. Of those that a mesh axis runs over, the one named last changes fastest.
Arguments:
- queries: bfloat16 [192, 4096], P('grp', 'side'), may hold values from -6 to 6
- kv_cache: bfloat16 [192, 16, 192, 256], P('grp', ('side', 'tp')), may hold values from -6 to 6
- lengths: int32 [192], P('grp'), may hold values from 2 to 768, as said below
- out_weight: bfloat16 [4096, 2048], P(('side', 'tp')), may hold values from -1 to 1
- resid: bfloat16 [192, 2048], P('grp'), may hold values from -6 to 6
- norm_gain: float32 [2048], replicated, may hold values from 0.1 to 1.9
- expert_ids: int32 [192, 8], P('grp'), may hold values from 0 to 127, all different within a row; in each aligned block of 24 rows (0 to 23, 24 to 47, ...) at most 3 rows name the same one
- expert_gates: float32 [192, 8], P('grp'), may hold values from 0.05 to 1
- w_gate_up: bfloat16 [128, 2048, 1536], P(('side', 'grp', 'tp')), may hold values from -0.125 to 0.125
- w_down: bfloat16 [128, 768, 2048], P(('side', 'grp', 'tp')), may hold values from -0.21875 to 0.21875
Outputs:
- layer_out: bfloat16 [192, 2048], P('grp', ('side', 'tp'))
Inputs may be any that keep to these rules, and one draw needn't show every extreme that they name: `lengths`: every row's cache holds at least two tokens; some row holds exactly 768. `expert_ids`: each row names 8 different experts. Among the rows of one row group no expert is named by more than 3 rows; in some group an expert is named by exactly 3.
All inputs are finite; a program needn't handle non-finite values.
Results may differ from a plain program's by a relative error of at most 0.017.
Values may be sent and summed in bfloat16 or wider, within the bound.
A program may use at most 64 MiB of HBM per device.

v0:
```python
import math
import jax
import jax.numpy as jnp
from jax import lax
from jax.sharding import PartitionSpec as P

QH = 32
KVH = 4
HD = 128
TOPK = 8


def swapped(value, axis, distance):
    mask = 2**distance
    pairs = [(source, source ^ mask) for source in range(lax.axis_size(axis))]
    return lax.ppermute(value, axis, pairs)


def body(
    queries,
    kv_cache,
    lengths,
    out_weight,
    resid,
    norm_gain,
    expert_ids,
    expert_gates,
    w_gate_up,
    w_down,
):
    lane_count = lax.axis_size("tp")
    tp_index = lax.axis_index("tp")
    side_count = lax.axis_size("side")
    section = lax.axis_index("side")
    grp_count = lax.axis_size("grp")
    group_size = side_count * lane_count
    member_index = section * lane_count + tp_index
    kv_parts = group_size // KVH
    group_heads = QH // KVH
    per_member = QH // group_size
    part_span = kv_cache.shape[2]
    model_width = out_weight.shape[1]
    piece_width = model_width // group_size
    rows_grp = lengths.shape[0]
    local_experts = w_gate_up.shape[0]
    experts_all = local_experts * side_count * grp_count * lane_count
    capacity = max(2, 2 * rows_grp * TOPK // experts_all)
    head_start = tp_index // kv_parts * group_heads * HD
    part_index = tp_index % kv_parts
    row_count = queries.shape[0]
    query_rows = lax.dynamic_slice_in_dim(queries, head_start, group_heads * HD, 1).reshape(
        row_count, group_heads, HD
    )
    key_rows = kv_cache[:, 0, :, :HD]
    value_rows = kv_cache[:, 0, :, HD:]
    positions = part_index * part_span + jnp.arange(part_span, dtype=jnp.int32)
    valid_mask = (positions[None, :] < lengths[:, None])[:, None, :]
    scores = jnp.einsum(
        "rgd,rpd->rgp", query_rows, key_rows, preferred_element_type=jnp.float32
    ) / math.sqrt(HD)
    scores = jnp.where(valid_mask, scores, -1e30)
    row_max = jnp.max(scores, axis=-1)
    for bit_index in range(kv_parts.bit_length() - 1):
        row_max = jnp.maximum(row_max, swapped(row_max, "tp", bit_index))
    weights = jnp.where(valid_mask, jnp.exp(scores - row_max[..., None]), 0.0)
    weight_sum = jnp.sum(weights, axis=-1)
    numerator = jnp.einsum(
        "rgp,rpd->rgd", weights.astype(jnp.bfloat16), value_rows, preferred_element_type=jnp.float32
    )
    for bit_index in range(kv_parts.bit_length() - 1):
        other_numerator, other_sum = swapped((numerator, weight_sum), "tp", bit_index)
        numerator = numerator + other_numerator
        weight_sum = weight_sum + other_sum
    heads_out = (numerator / weight_sum[..., None]).astype(jnp.bfloat16)
    mine = lax.dynamic_slice_in_dim(heads_out, part_index * per_member, per_member, 1).reshape(
        row_count, per_member * HD
    )
    projected = jnp.dot(mine, out_weight, preferred_element_type=jnp.float32)
    summed = lax.psum(projected, ("side", "tp"))
    middle = (resid.astype(jnp.float32) + summed).astype(jnp.bfloat16)
    middle_wide = middle.astype(jnp.float32)
    inv_rms = lax.rsqrt(jnp.mean(middle_wide * middle_wide, axis=-1, keepdims=True) + 1e-06)
    normed = (middle_wide * inv_rms * norm_gain).astype(jnp.bfloat16)
    column_experts = (
        (
            (section * grp_count + jnp.arange(grp_count, dtype=jnp.int32)[:, None]) * lane_count
            + tp_index
        )
        * local_experts
        + jnp.arange(local_experts, dtype=jnp.int32)[None, :]
    ).reshape(-1)
    matches = expert_ids[:, :, None] == column_experts[None, None, :]
    hit_count = jnp.sum(matches.astype(jnp.int32), axis=1)
    gate_cols = jnp.sum(jnp.where(matches, expert_gates[:, :, None], 0.0), axis=1)
    slot_rank = jnp.cumsum(hit_count, axis=0) - hit_count
    slot_ids = jnp.arange(capacity, dtype=jnp.int32)
    placed = (hit_count[:, :, None] == 1) & (slot_rank[:, :, None] == slot_ids[None, None, :])
    send_map = placed.astype(jnp.bfloat16)
    outgoing = jnp.einsum(
        "rcs,rd->csd", send_map, normed, preferred_element_type=jnp.float32
    ).astype(jnp.bfloat16)
    outgoing = outgoing.reshape(grp_count, local_experts, capacity, model_width)
    hidden = jnp.einsum(
        "gjcd,jdf->gjcf",
        lax.all_to_all(outgoing, "grp", split_axis=0, concat_axis=0, tiled=True),
        w_gate_up,
        preferred_element_type=jnp.float32,
    )
    inner_width = hidden.shape[-1] // 2
    activated = (jax.nn.silu(hidden[..., :inner_width]) * hidden[..., inner_width:]).astype(
        jnp.bfloat16
    )
    produced = jnp.einsum(
        "gjcf,jfd->gjcd", activated, w_down, preferred_element_type=jnp.float32
    ).astype(jnp.bfloat16)
    returned = lax.all_to_all(produced, "grp", split_axis=0, concat_axis=0, tiled=True)
    combine_weights = (send_map.astype(jnp.float32) * gate_cols[:, :, None]).reshape(row_count, -1)
    moe_part = jnp.dot(
        combine_weights,
        returned.reshape(-1, model_width).astype(jnp.float32),
        precision=lax.Precision.HIGHEST,
    )
    middle_mine = lax.dynamic_slice_in_dim(middle_wide, member_index * piece_width, piece_width, 1)
    moe_whole = lax.psum(moe_part, ("side", "tp"))
    return (
        middle_mine
        + lax.dynamic_slice_in_dim(moe_whole, member_index * piece_width, piece_width, 1)
    ).astype(jnp.bfloat16)


def solution(mesh):
    in_specs = (
        P("grp", "side"),
        P("grp", ("side", "tp"), None, None),
        P("grp"),
        P(("side", "tp"), None),
        P("grp", None),
        P(),
        P("grp", None),
        P("grp", None),
        P(("side", "grp", "tp"), None, None),
        P(("side", "grp", "tp"), None, None),
    )
    out_specs = P("grp", ("side", "tp"))
    return jax.shard_map(body, mesh=mesh, in_specs=in_specs, out_specs=out_specs, check_vma=False)
```

profile of v0, /device:TPU:1, one launch (start us, length us, event | category | flops | bytes accessed | tf_op | source)
XLA Modules:
  0.0 333.3 jit_solution(7118665528007655057)
XLA Ops:
  6.5 0.0 copy-start
  6.5 0.0 copy-start.3
  6.5 0.0 all-reduce.3.cloned.1.call-start
  6.6 1.0 dynamic-slice_bitcast_fusion
  7.5 0.7 broadcast_compare_fusion
  8.3 0.0 copy-start.1
  8.3 2.1 fusion.47
  10.3 2.5 collective-permute-start
  12.8 0.8 fusion.34
  13.6 0.3 collective-permute-done
  13.9 3.4 %collective-permute-start.1 = (f32[24,8]{1,0:T(8,128)S(1)}, f32[24,8]{1,0:T(8,128)S(1)}, u32[]{:S(2)}, u32[]{:S(2)}) collective-permute-start(f32[24,8]{1,0:T(8,128)S(1)} %max.6), channel_id=1, source_target_pairs={{0,2},{1,3},{2,0},{3,1},{4,6},{5,7},{6,4},{7,5},{8,10},{9,11},{10,... | collective-permute-start | bytes 2312 | tf_op jit(solution)/shard_map/ppermute | solution.py:16
  17.3 0.6 broadcast_compare_fusion.1
  17.9 0.6 collective-permute-done.1
  18.5 0.2 fusion.18
  18.7 1.0 collective-permute-start.4
  19.7 1.7 fusion.14
  21.4 0.5 collective-permute-start.2
  22.0 0.0 collective-permute-done.4
  22.0 2.9 collective-permute-start.5
  24.9 0.0 copy-done.3
  24.9 0.8 fusion.35
  25.7 0.1 copy.37
  25.8 0.1 copy.39
  25.9 1.1 collective-permute-done.5
  27.0 0.0 collective-permute-done.2
  27.0 2.0 collective-permute-start.3
  29.1 0.1 constant_dynamic-slice_fusion
  29.1 2.9 collective-permute-done.3
  32.1 0.1 fusion.37
  32.2 2.2 fusion.39
  34.4 0.0 all-reduce.3.cloned.1.call-update
  34.4 1.3 convert_multiply_fusion
  35.7 130.8 %all-reduce.3.cloned.1.call-done = f32[24,2048]{1,0:T(8,128)} async-done(((f32[24,2048]{1,0:T(8,128)}), f32[24,2048]{1,0:T(8,128)}) %all-reduce.3.cloned.1.call-update) | async-done | bytes 196624 | tf_op jit(solution)/shard_map/psum | solution.py:79
  166.5 0.0 copy-done.1
  166.5 1.1 multiply_reduce_fusion
  167.5 0.9 fusion.10
  168.5 0.1 copy.41
  168.6 13.4 %all_to_all.10 = bf16[8,1,3,2048]{3,2,1,0:T(4,128)(2,1)S(1)} all-to-all(bf16[8,1,3,2048]{3,2,1,0:T(4,128)(2,1)S(1)} %copy.41), channel_id=1, replica_groups=mesh['side'=2,'grp'=8,'tp'=8] {'grp'}, dimensions={0} | all-to-all | bytes 196608 | tf_op jit(solution)/shard_map/all_to_all | solution.py:105
  182.0 3.7 %fusion.4 = f32[8,1,3,1536]{3,0,2,1:T(8,128)S(1)} fusion(bf16[1,2048,1536]{2,1,0:T(8,128)(2,1)} %param.18, bf16[8,1,3,2048]{3,2,1,0:T(4,128)(2,1)S(1)} %all_to_all.10), kind=kOutput, calls=%fused_computation.4 | convolution fusion | flops 150994944 | bytes 6537216 | tf_op jit(solution)/shard_map/gjcd,jdf->gjcf/dot_general | solution.py:103
  185.7 0.0 copy-done
  185.7 0.0 copy-start.2
  185.7 0.5 fusion.11
  186.2 0.7 copy.43
  187.0 3.4 %all-to-all-start.1 = ((bf16[8,1,3,2048]{3,2,1,0:T(4,128)(2,1)}), bf16[8,1,3,2048]{3,2,1,0:T(4,128)(2,1)S(1)}, u32[]{:S(2)}, u32[]{:S(2)}) async-start(bf16[8,1,3,2048]{3,2,1,0:T(4,128)(2,1)} %copy.43), calls=%async_computation.1 | async-start | bytes 262144 | tf_op jit(solution)/shard_map/all_to_all | solution.py:116
  190.3 0.0 all-reduce.5.cloned.1.call-start
  190.4 0.0 copy-done.2
  190.4 6.8 %all-to-all-done.1 = bf16[8,1,3,2048]{3,2,1,0:T(4,128)(2,1)S(1)} async-done(((bf16[8,1,3,2048]{3,2,1,0:T(4,128)(2,1)}), bf16[8,1,3,2048]{3,2,1,0:T(4,128)(2,1)S(1)}, u32[]{:S(2)}, u32[]{:S(2)}) %all-to-all-start.1) | async-done | bytes 98336 | tf_op jit(solution)/shard_map/all_to_all | solution.py:116
  197.2 0.7 reshape.139
  197.9 1.9 fusion.48
  199.8 0.0 all-reduce.5.cloned.1.call-update
  199.8 125.3 %all-reduce.5.cloned.1.call-done = f32[24,2048]{1,0:T(8,128)} async-done(((f32[24,2048]{1,0:T(8,128)}), f32[24,2048]{1,0:T(8,128)}) %all-reduce.5.cloned.1.call-update) | async-done | bytes 196624 | tf_op jit(solution)/shard_map/psum | solution.py:124
  325.1 1.3 add_convert_fusion.1
  (12 shorter events, 0.1 us)
Async XLA Ops:
  6.5 179.2 %copy-start = (bf16[1,768,2048]{2,1,0:T(8,128)(2,1)S(1)}, bf16[1,768,2048]{2,1,0:T(8,128)(2,1)}, u32[]{:S(2)}) copy-start(bf16[1,768,2048]{2,1,0:T(8,128)(2,1)} %param.19) | copy-start | bytes 9437188
  6.5 18.4 %copy-start.3 = (s32[24,8]{0,1:T(8,128)S(1)}, s32[24,8]{0,1:T(8,128)}, u32[]{:S(2)}) copy-start(s32[24,8]{0,1:T(8,128)} %param.16) | copy-start | bytes 2308
  6.5 159.9 %all-reduce.3.cloned.1.call-start = ((), (), s32[]{:S(2)}) async-start(), calls=%async_computation.2 | async-start | bytes 393216 | tf_op jit(solution)/shard_map/psum | solution.py:79
  8.3 158.2 %copy-start.1 = (bf16[24,2048]{1,0:T(8,128)(2,1)S(1)}, bf16[24,2048]{1,0:T(8,128)(2,1)}, u32[]{:S(2)}) copy-start(bf16[24,2048]{1,0:T(8,128)(2,1)} %param.14) | copy-start | bytes 294916
  10.3 3.6 %collective-permute-start = (f32[24,8]{1,0:T(8,128)S(1)}, f32[24,8]{1,0:T(8,128)S(1)}, u32[]{:S(2)}, u32[]{:S(2)}) collective-permute-start(f32[24,8]{1,0:T(8,128)S(1)} %get-tuple-element.9), channel_id=1, source_target_pairs={{0,1},{1,0},{2,3},{3,2},{4,5},{5,4},{6,7},{7,6},{8,9},{9,8},{10,11... | collective-permute-start | bytes 2312 | tf_op jit(solution)/shard_map/ppermute | solution.py:16
  13.9 4.6 %collective-permute-start.1 = (f32[24,8]{1,0:T(8,128)S(1)}, f32[24,8]{1,0:T(8,128)S(1)}, u32[]{:S(2)}, u32[]{:S(2)}) collective-permute-start(f32[24,8]{1,0:T(8,128)S(1)} %max.6), channel_id=1, source_target_pairs={{0,2},{1,3},{2,0},{3,1},{4,6},{5,7},{6,4},{7,5},{8,10},{9,11},{10,... | collective-permute-start | bytes 2312 | tf_op jit(solution)/shard_map/ppermute | solution.py:16
  18.7 3.3 collective-permute-start.4
  21.4 5.6 %collective-permute-start.2 = (f32[24,8,128]{2,1,0:T(8,128)S(1)}, f32[24,8,128]{2,1,0:T(8,128)S(1)}, u32[]{:S(2)}, u32[]{:S(2)}) collective-permute-start(f32[24,8,128]{2,1,0:T(8,128)S(1)} %fusion.14), channel_id=1, source_target_pairs={{0,1},{1,0},{2,3},{3,2},{4,5},{5,4},{6,7},{7,6},{8,9},{9,8},{10,11... | collective-permute-start | bytes 294920 | tf_op jit(solution)/shard_map/ppermute | solution.py:16
  22.0 5.0 %collective-permute-start.5 = (f32[24,8]{1,0:T(8,128)S(1)}, f32[24,8]{1,0:T(8,128)S(1)}, u32[]{:S(2)}, u32[]{:S(2)}) collective-permute-start(f32[24,8]{1,0:T(8,128)S(1)} %add.92), channel_id=1, source_target_pairs={{0,2},{1,3},{2,0},{3,1},{4,6},{5,7},{6,4},{7,5},{8,10},{9,11},{10,... | collective-permute-start | bytes 2312 | tf_op jit(solution)/shard_map/ppermute | solution.py:16
  27.0 5.1 %collective-permute-start.3 = (f32[24,8,128]{2,1,0:T(8,128)S(1)}, f32[24,8,128]{2,1,0:T(8,128)S(1)}, u32[]{:S(2)}, u32[]{:S(2)}) collective-permute-start(f32[24,8,128]{2,1,0:T(8,128)S(1)} %add.90), channel_id=1, source_target_pairs={{0,2},{1,3},{2,0},{3,1},{4,6},{5,7},{6,4},{7,5},{8,10},{9,11},{10,... | collective-permute-start | bytes 294920 | tf_op jit(solution)/shard_map/ppermute | solution.py:16
  185.7 4.7 %copy-start.2 = (f32[24,8,3]{0,2,1:T(4,128)S(1)}, f32[24,8,3]{0,2,1:T(4,128)}, u32[]{:S(2)}) copy-start(f32[24,8,3]{0,2,1:T(4,128)} %get-tuple-element.7) | copy-start | bytes 6916
  187.0 10.3 %all-to-all-start.1 = ((bf16[8,1,3,2048]{3,2,1,0:T(4,128)(2,1)}), bf16[8,1,3,2048]{3,2,1,0:T(4,128)(2,1)S(1)}, u32[]{:S(2)}, u32[]{:S(2)}) async-start(bf16[8,1,3,2048]{3,2,1,0:T(4,128)(2,1)} %copy.43), calls=%async_computation.1 | async-start | bytes 262144 | tf_op jit(solution)/shard_map/all_to_all | solution.py:116
  190.3 134.8 %all-reduce.5.cloned.1.call-start = ((), (), s32[]{:S(2)}) async-start(), calls=%async_computation.3 | async-start | bytes 393216 | tf_op jit(solution)/shard_map/psum | solution.py:124
Sparse Core Ops, SparseCore 0:
  34.5 131.9 all-reduce.2
  199.9 125.1 all-reduce.4
where the time goes:
time: 334 us; the launch traced here: 333 us
  waiting for transfers between devices  268 us (80%)
  starting transfers between devices  15.9 us (5%)
  between operations  13.5 us (4%)
  blocking collectives  13.4 us (4%)
  matrix products  13 us (4%)
  other arithmetic  6.89 us (2%)
    psum x1, waiting for transfers between devices, body(): summed = lax.psum(projected, ('side', 'tp'))  131 us
    psum x1, waiting for transfers between devices, body(): moe_whole = lax.psum(moe_part, ('side', 'tp'))  125 us
    all_to_all x1, blocking collectives, body(): lax.all_to_all(outgoing, 'grp', split_axis=0, concat_axis=0, tiled=True)  13.4 us
    ppermute x6, starting transfers between devices, swapped(): return lax.ppermute(value, axis, pairs)  12.4 us
    all_to_all x1, waiting for transfers between devices, body(): lax.all_to_all(produced, 'grp', split_axis=0, concat_axis=0, tiled=True)  6.8 us
  transfers between devices with their start and end apart: 9, of which 7 were waited for; matrix products, arithmetic and copies ran while one was open for 2% of the time, Pallas kernels for 0%

commit v1 on v0

--- a/solution.py
+++ b/solution.py
@@ -76,7 +76,8 @@
         row_count, per_member * HD
     )
     projected = jnp.dot(mine, out_weight, preferred_element_type=jnp.float32)
-    summed = lax.psum(projected, ("side", "tp"))
+    shards = lax.all_gather(projected, ("side", "tp"), axis=0, tiled=False)
+    summed = shards.sum(axis=0)
     middle = (resid.astype(jnp.float32) + summed).astype(jnp.bfloat16)
     middle_wide = middle.astype(jnp.float32)
     inv_rms = lax.rsqrt(jnp.mean(middle_wide * middle_wide, axis=-1, keepdims=True) + 1e-06)

time: 334 us -> 248 us (0.74)
  waiting for transfers between devices: 268 us -> 182 us
    psum x1 -> x0, waiting for transfers between devices: 131 us -> none  [body(): summed = lax.psum(projected, ('side', 'tp'))]
    all_gather x0 -> x1, waiting for transfers between devices: none -> 43.3 us  [body(): shards = lax.all_gather(projected, ('side', 'tp'), axis=0, tiled=False)]
  transfers between devices with their start and end apart: 9 -> 9, of which waited for: 7 -> 8; matrix products, arithmetic and copies ran while one was open for 2% -> 1% of each run, Pallas kernels for 0% -> 0%
where the time goes in v1:
time: 248 us
  waiting for transfers between devices  182 us (73%)
  starting transfers between devices  17.2 us (7%)
  between operations  13.5 us (5%)
  matrix products  13 us (5%)
  blocking collectives  12.9 us (5%)
  other arithmetic  6.28 us (3%)
  local copies, waits for them, and re-layouts  2.75 us (1%)
    psum x1, waiting for transfers between devices, body(): moe_whole = lax.psum(moe_part, ('side', 'tp'))  125 us
    all_gather x1, waiting for transfers between devices, body(): shards = lax.all_gather(projected, ('side', 'tp'), axis=0, tiled=False)  43.3 us
    ppermute x6, starting transfers between devices, swapped(): return lax.ppermute(value, axis, pairs)  13.8 us
    all_to_all x1, blocking collectives, body(): lax.all_to_all(outgoing, 'grp', split_axis=0, concat_axis=0, tiled=True)  12.9 us
    ppermute x6, waiting for transfers between devices, swapped(): return lax.ppermute(value, axis, pairs)  7.4 us
    all_to_all x1, waiting for transfers between devices, body(): lax.all_to_all(produced, 'grp', split_axis=0, concat_axis=0, tiled=True)  6.81 us
  transfers between devices with their start and end apart: 9, of which 8 were waited for; matrix products, arithmetic and copies ran while one was open for 1% of the time, Pallas kernels for 0%

profile of v1, /device:TPU:1, one launch (start us, length us, event | category | flops | bytes accessed | tf_op | source)
XLA Modules:
  0.0 247.7 jit_solution(8369777246671961106)
XLA Ops:
  6.5 0.0 copy-start
  6.5 0.0 copy-start.1
  6.5 0.0 copy-start.2
  6.5 0.0 all-gather.3.cloned.1.call-start
  6.6 1.0 dynamic-slice_bitcast_fusion
  7.6 0.7 broadcast_compare_fusion
  8.3 2.1 fusion.47
  10.4 2.5 %collective-permute-start = (f32[24,8]{1,0:T(8,128)S(1)}, f32[24,8]{1,0:T(8,128)S(1)}, u32[]{:S(2)}, u32[]{:S(2)}) collective-permute-start(f32[24,8]{1,0:T(8,128)S(1)} %get-tuple-element.9), channel_id=1, source_target_pairs={{0,1},{1,0},{2,3},{3,2},{4,5},{5,4},{6,7},{7,6},{8,9},{9,8},{10,11... | collective-permute-start | bytes 2312 | tf_op jit(solution)/shard_map/ppermute | solution.py:16
  12.8 1.1 collective-permute-done
  13.9 3.4 %collective-permute-start.1 = (f32[24,8]{1,0:T(8,128)S(1)}, f32[24,8]{1,0:T(8,128)S(1)}, u32[]{:S(2)}, u32[]{:S(2)}) collective-permute-start(f32[24,8]{1,0:T(8,128)S(1)} %max.6), channel_id=1, source_target_pairs={{0,2},{1,3},{2,0},{3,1},{4,6},{5,7},{6,4},{7,5},{8,10},{9,11},{10,... | collective-permute-start | bytes 2312 | tf_op jit(solution)/shard_map/ppermute | solution.py:16
  17.3 1.1 collective-permute-done.1
  18.5 1.7 fusion.14
  20.2 1.0 collective-permute-start.2
  21.2 0.2 fusion.18
  21.4 0.6 collective-permute-start.4
  22.0 2.0 collective-permute-done.4
  24.0 3.3 %collective-permute-start.5 = (f32[24,8]{1,0:T(8,128)S(1)}, f32[24,8]{1,0:T(8,128)S(1)}, u32[]{:S(2)}, u32[]{:S(2)}) collective-permute-start(f32[24,8]{1,0:T(8,128)S(1)} %add.90), channel_id=1, source_target_pairs={{0,2},{1,3},{2,0},{3,1},{4,6},{5,7},{6,4},{7,5},{8,10},{9,11},{10,... | collective-permute-start | bytes 2312 | tf_op jit(solution)/shard_map/ppermute | solution.py:16
  27.3 1.1 collective-permute-done.5
  28.4 0.0 collective-permute-done.2
  28.4 3.0 %collective-permute-start.3 = (f32[24,8,128]{2,1,0:T(8,128)S(1)}, f32[24,8,128]{2,1,0:T(8,128)S(1)}, u32[]{:S(2)}, u32[]{:S(2)}) collective-permute-start(f32[24,8,128]{2,1,0:T(8,128)S(1)} %add.88), channel_id=1, source_target_pairs={{0,2},{1,3},{2,0},{3,1},{4,6},{5,7},{6,4},{7,5},{8,10},{9,11},{10,... | collective-permute-start | bytes 294920 | tf_op jit(solution)/shard_map/ppermute | solution.py:16
  31.5 0.1 constant_dynamic-slice_fusion
  31.5 2.1 collective-permute-done.3
  33.6 0.1 fusion.37
  33.7 2.2 fusion.39
  35.9 0.0 all-gather.3.cloned.1.call-update
  35.9 0.0 copy-done.1
  35.9 0.1 fusion.34
  36.0 0.1 copy.37
  36.1 0.1 copy.39
  36.2 0.0 copy-done.2
  36.2 0.1 fusion.35
  36.3 0.6 convert_multiply_fusion
  36.9 43.3 %all-gather.3.cloned.1.call-done = f32[384,2048]{1,0:T(8,128)} async-done(((f32[24,2048]{1,0:T(8,128)}), f32[384,2048]{1,0:T(8,128)}) %all-gather.3.cloned.1.call-update) | async-done | bytes 3145744 | tf_op jit(solution)/shard_map/all_gather | solution.py:79
  80.2 2.1 reduce_sum.46
  82.2 1.0 multiply_reduce_fusion
  83.3 0.9 fusion.10
  84.2 0.1 copy.41
  84.3 12.9 %all_to_all.10 = bf16[8,1,3,2048]{3,2,1,0:T(4,128)(2,1)S(1)} all-to-all(bf16[8,1,3,2048]{3,2,1,0:T(4,128)(2,1)S(1)} %copy.41), channel_id=1, replica_groups=mesh['side'=2,'grp'=8,'tp'=8] {'grp'}, dimensions={0} | all-to-all | bytes 196608 | tf_op jit(solution)/shard_map/all_to_all | solution.py:106
  97.2 3.7 %fusion.4 = f32[8,1,3,1536]{3,0,2,1:T(8,128)S(1)} fusion(bf16[1,2048,1536]{2,1,0:T(8,128)(2,1)} %param.18, bf16[8,1,3,2048]{3,2,1,0:T(4,128)(2,1)S(1)} %all_to_all.10), kind=kOutput, calls=%fused_computation.4 | convolution fusion | flops 150994944 | bytes 6537216 | tf_op jit(solution)/shard_map/gjcd,jdf->gjcf/dot_general | solution.py:104
  100.9 0.0 copy-done
  100.9 0.5 fusion.11
  101.5 0.7 copy.43
  102.2 3.4 %all-to-all-start.1 = ((bf16[8,1,3,2048]{3,2,1,0:T(4,128)(2,1)}), bf16[8,1,3,2048]{3,2,1,0:T(4,128)(2,1)S(1)}, u32[]{:S(2)}, u32[]{:S(2)}) async-start(bf16[8,1,3,2048]{3,2,1,0:T(4,128)(2,1)} %copy.43), calls=%async_computation.1 | async-start | bytes 262144 | tf_op jit(solution)/shard_map/all_to_all | solution.py:117
  105.6 0.0 all-reduce.2.cloned.1.call-start
  105.6 6.8 %all-to-all-done.1 = bf16[8,1,3,2048]{3,2,1,0:T(4,128)(2,1)S(1)} async-done(((bf16[8,1,3,2048]{3,2,1,0:T(4,128)(2,1)}), bf16[8,1,3,2048]{3,2,1,0:T(4,128)(2,1)S(1)}, u32[]{:S(2)}, u32[]{:S(2)}) %all-to-all-start.1) | async-done | bytes 98336 | tf_op jit(solution)/shard_map/all_to_all | solution.py:117
  112.5 0.7 reshape.139
  113.2 1.8 fusion.48
  115.0 0.0 all-reduce.2.cloned.1.call-update
  115.0 124.5 %all-reduce.2.cloned.1.call-done = f32[24,2048]{1,0:T(8,128)} async-done(((f32[24,2048]{1,0:T(8,128)}), f32[24,2048]{1,0:T(8,128)}) %all-reduce.2.cloned.1.call-update) | async-done | bytes 196624 | tf_op jit(solution)/shard_map/psum | solution.py:125
  239.6 1.3 add_convert_fusion.1
  (13 shorter events, 0.1 us)
Async XLA Ops:
  6.5 94.4 %copy-start = (bf16[1,768,2048]{2,1,0:T(8,128)(2,1)S(1)}, bf16[1,768,2048]{2,1,0:T(8,128)(2,1)}, u32[]{:S(2)}) copy-start(bf16[1,768,2048]{2,1,0:T(8,128)(2,1)} %param.19) | copy-start | bytes 9437188
  6.5 29.4 %copy-start.1 = (s32[24,8]{0,1:T(8,128)S(1)}, s32[24,8]{0,1:T(8,128)}, u32[]{:S(2)}) copy-start(s32[24,8]{0,1:T(8,128)} %param.16) | copy-start | bytes 2308
  6.5 29.7 %copy-start.2 = (f32[24,8]{0,1:T(8,128)S(1)}, f32[24,8]{0,1:T(8,128)}, u32[]{:S(2)}) copy-start(f32[24,8]{0,1:T(8,128)} %param.17) | copy-start | bytes 2308
  6.5 73.6 %all-gather.3.cloned.1.call-start = ((), (), s32[]{:S(2)}) async-start(), calls=%async_computation.3 | async-start | bytes 3342336 | tf_op jit(solution)/shard_map/all_gather | solution.py:79
  10.4 3.6 %collective-permute-start = (f32[24,8]{1,0:T(8,128)S(1)}, f32[24,8]{1,0:T(8,128)S(1)}, u32[]{:S(2)}, u32[]{:S(2)}) collective-permute-start(f32[24,8]{1,0:T(8,128)S(1)} %get-tuple-element.9), channel_id=1, source_target_pairs={{0,1},{1,0},{2,3},{3,2},{4,5},{5,4},{6,7},{7,6},{8,9},{9,8},{10,11... | collective-permute-start | bytes 2312 | tf_op jit(solution)/shard_map/ppermute | solution.py:16
  13.9 4.6 %collective-permute-start.1 = (f32[24,8]{1,0:T(8,128)S(1)}, f32[24,8]{1,0:T(8,128)S(1)}, u32[]{:S(2)}, u32[]{:S(2)}) collective-permute-start(f32[24,8]{1,0:T(8,128)S(1)} %max.6), channel_id=1, source_target_pairs={{0,2},{1,3},{2,0},{3,1},{4,6},{5,7},{6,4},{7,5},{8,10},{9,11},{10,... | collective-permute-start | bytes 2312 | tf_op jit(solution)/shard_map/ppermute | solution.py:16
  20.2 8.2 %collective-permute-start.2 = (f32[24,8,128]{2,1,0:T(8,128)S(1)}, f32[24,8,128]{2,1,0:T(8,128)S(1)}, u32[]{:S(2)}, u32[]{:S(2)}) collective-permute-start(f32[24,8,128]{2,1,0:T(8,128)S(1)} %fusion.14), channel_id=1, source_target_pairs={{0,1},{1,0},{2,3},{3,2},{4,5},{5,4},{6,7},{7,6},{8,9},{9,8},{10,11... | collective-permute-start | bytes 294920 | tf_op jit(solution)/shard_map/ppermute | solution.py:16
  21.4 2.6 %collective-permute-start.4 = (f32[24,8]{1,0:T(8,128)S(1)}, f32[24,8]{1,0:T(8,128)S(1)}, u32[]{:S(2)}, u32[]{:S(2)}) collective-permute-start(f32[24,8]{1,0:T(8,128)S(1)} %fusion.18), channel_id=1, source_target_pairs={{0,1},{1,0},{2,3},{3,2},{4,5},{5,4},{6,7},{7,6},{8,9},{9,8},{10,11... | collective-permute-start | bytes 2312 | tf_op jit(solution)/shard_map/ppermute | solution.py:16
  24.0 4.4 %collective-permute-start.5 = (f32[24,8]{1,0:T(8,128)S(1)}, f32[24,8]{1,0:T(8,128)S(1)}, u32[]{:S(2)}, u32[]{:S(2)}) collective-permute-start(f32[24,8]{1,0:T(8,128)S(1)} %add.90), channel_id=1, source_target_pairs={{0,2},{1,3},{2,0},{3,1},{4,6},{5,7},{6,4},{7,5},{8,10},{9,11},{10,... | collective-permute-start | bytes 2312 | tf_op jit(solution)/shard_map/ppermute | solution.py:16
  28.4 5.2 %collective-permute-start.3 = (f32[24,8,128]{2,1,0:T(8,128)S(1)}, f32[24,8,128]{2,1,0:T(8,128)S(1)}, u32[]{:S(2)}, u32[]{:S(2)}) collective-permute-start(f32[24,8,128]{2,1,0:T(8,128)S(1)} %add.88), channel_id=1, source_target_pairs={{0,2},{1,3},{2,0},{3,1},{4,6},{5,7},{6,4},{7,5},{8,10},{9,11},{10,... | collective-permute-start | bytes 294920 | tf_op jit(solution)/shard_map/ppermute | solution.py:16
  102.2 10.2 %all-to-all-start.1 = ((bf16[8,1,3,2048]{3,2,1,0:T(4,128)(2,1)}), bf16[8,1,3,2048]{3,2,1,0:T(4,128)(2,1)S(1)}, u32[]{:S(2)}, u32[]{:S(2)}) async-start(bf16[8,1,3,2048]{3,2,1,0:T(4,128)(2,1)} %copy.43), calls=%async_computation.1 | async-start | bytes 262144 | tf_op jit(solution)/shard_map/all_to_all | solution.py:117
  105.6 134.0 %all-reduce.2.cloned.1.call-start = ((), (), s32[]{:S(2)}) async-start(), calls=%async_computation.2 | async-start | bytes 393216 | tf_op jit(solution)/shard_map/psum | solution.py:125
Sparse Core Ops, SparseCore 0:
  36.0 44.1 all-gather.2
  115.2 124.3 all-reduce.1
